TPU v7x, 32 devices: a whole 2x2x4 slice. The times are simulated.
32 devices in a mesh: row: 4 (over z), col: 2 (over x), pole: 4 (over y, core).
Axes of the slice: x: 2, y: 2, z: 4, core: 2. Of those that a mesh axis runs over, the one named last changes fastest.
Arguments:
- window: bfloat16 [4, 8192, 8192], P('pole', 'col', 'row'), may hold values from -6 to 6
- panels: bfloat16 [4, 2, 8192, 256], P('pole', 'col', 'row'), may hold values from -0.0625 to 0.0625
- row_map: int32 [3, 8192], P(None, 'row'), may hold values from 0 to 8191, as said below
- panel_root: int32 [4, 3], P('pole'), may hold values from 0 to 1
- upper_blocks: bfloat16 [4, 3, 256, 256], P('pole', None, 'row'), may hold values from -0.375 to 0.375
- diag_inverse: float32 [4, 3, 256, 256], P('pole', None, 'row'), may hold values from -6 to 6
- weights: float32 [4], replicated, may hold values from 0.25 to 1
- pole_order: int32 [4], P('pole'), may hold values from 0 to 3, each once
Outputs:
- inv_columns: float32 [3, 2, 4096, 256], P(None, 'col', ('row', 'pole'))
- inv_diag: float32 [3, 256, 256], P(None, ('row', 'pole'))
Inputs may be any that keep to these rules, and one draw needn't show every extreme that they name: row_map[k] permutes the positions inside each aligned group of 1024 consecutive positions. `pole_order`: each of the 4 poles appears once.
All inputs are finite; a program needn't handle non-finite values.
Results may differ from a plain program's by a relative error of at most 0.0003.
Values may be sent and summed in bfloat16 or wider, within the bound.
A program may use at most 128 MiB of HBM per device.

v0:
```python
import jax
import jax.numpy as jnp
from jax import lax
from jax.sharding import PartitionSpec as P

NS = 3


def precise(left, right):
    return jnp.dot(left, right, precision=lax.Precision.HIGHEST, preferred_element_type=jnp.float32)


def pair_index(current, earlier):
    return current * (current - 1) // 2 + earlier


def inverse_block(diagonals, crossed, first, second):
    if first == second:
        return diagonals[first]
    if first < second:
        return crossed[first, second]
    return crossed[second, first].T


def window_term(window_block, aligned):
    return jnp.dot(window_block, aligned, preferred_element_type=jnp.float32)


def shards(window, panels, row_map, panel_root, upper_blocks, diag_inverse, weights, pole_order):
    window_block = window[0]
    panel_slab = panels[0, 0]
    pole_roots = panel_root[0]
    band_rows = panel_slab.shape[0]
    group_rows = window_block.shape[0] // lax.axis_size("row")
    row_index = lax.axis_index("row")
    col_index = lax.axis_index("col")
    gathered_upper, gathered_inverse = (
        lax.all_gather(upper_blocks.astype(jnp.float32), "row", axis=2, tiled=True).astype(
            upper_blocks.dtype
        ),
        lax.all_gather(diag_inverse, "row", axis=2, tiled=True),
    )
    factors = gathered_upper[0].astype(jnp.float32)
    inverses = gathered_inverse[0]
    share_rows = inverses.shape[1] // lax.axis_size("row")
    slot_panels = lax.all_gather(panels, "col", axis=1, tiled=True)[0]
    pole_weight = jnp.sum(jnp.where(jnp.arange(weights.shape[0]) == pole_order[0], weights, 0.0))
    columns = []
    diagonals = []
    crossed = {}
    for current in range(NS):
        received = lax.dynamic_index_in_dim(slot_panels, pole_roots[current], 0, keepdims=False)
        aligned = jnp.take(received, row_map[current] - row_index * band_rows, axis=0)
        own_rows = lax.dynamic_slice_in_dim(aligned, col_index * group_rows, group_rows, 0).astype(
            jnp.float32
        )
        partials = [precise(columns[earlier].T, own_rows) for earlier in range(current)]
        window_sum = lax.psum_scatter(
            window_term(window_block, aligned), "row", scatter_dimension=0, tiled=True
        )
        y_window = window_sum
        for earlier in range(current):
            y_window = y_window + precise(columns[earlier], factors[pair_index(current, earlier)])
        congruence = precise(own_rows.T, y_window)
        stacked = lax.psum(jnp.stack(partials + [congruence]), ("row", "col"))
        summed_cross = stacked[:current]
        summed_own = stacked[current]
        y_blocks = []
        for earlier in range(current):
            block_sum = summed_cross[earlier]
            for other_node in range(current):
                block_sum = block_sum + precise(
                    inverse_block(diagonals, crossed, earlier, other_node),
                    factors[pair_index(current, other_node)],
                )
            y_blocks.append(block_sum)
        diagonal = inverses[current] + summed_own
        for earlier in range(current):
            diagonal = diagonal + precise(
                factors[pair_index(current, earlier)].T, y_blocks[earlier]
            )
            crossed[earlier, current] = -y_blocks[earlier]
        columns.append(-y_window)
        diagonals.append(diagonal)
    column_terms = jnp.stack(columns) * pole_weight
    diagonal_terms = (
        jnp.stack(
            [
                lax.dynamic_slice_in_dim(diagonal, row_index * share_rows, share_rows, 0)
                for diagonal in diagonals
            ]
        )
        * pole_weight
    )
    summed_columns, summed_diagonals = (
        lax.psum_scatter(column_terms, "pole", scatter_dimension=1, tiled=True),
        lax.psum_scatter(diagonal_terms, "pole", scatter_dimension=1, tiled=True),
    )
    return (summed_columns[:, None], summed_diagonals)


def solution(mesh):
    return jax.shard_map(
        shards,
        mesh=mesh,
        in_specs=(
            P("pole", "col", "row"),
            P("pole", "col", "row", None),
            P(None, "row"),
            P("pole", None),
            P("pole", None, "row", None),
            P("pole", None, "row", None),
            P(),
            P("pole"),
        ),
        out_specs=(P(None, "col", ("row", "pole"), None), P(None, ("row", "pole"), None)),
        check_vma=False,
    )
```

profile of v0, /device:TPU:0, one launch (start us, length us, event | category | flops | bytes accessed | tf_op | source)
XLA Modules:
  0.0 490.8 jit_solution(11846383781759528025)
XLA Ops:
  7.2 0.7 all-gather.2.cloned.1.call-update
  7.9 1.4 fusion.45
  15.1 0.9 slice_subtract_fusion.1
  16.0 29.3 %all-gather.2.cloned.1.call-done = bf16[1,2,2048,256]{3,2,0,1:T(8,128)(2,1)} async-done(((bf16[1,1,2048,256]{3,2,0,1:T(8,128)(2,1)}), bf16[1,2,2048,256]{3,2,0,1:T(8,128)(2,1)}) %all-gather.2.cloned.1.call-update) | async-done | bytes 2097168 | tf_op jit(solution)/shard_map/all_gather | solution.py:46
  45.4 2.2 dynamic-slice_bitcast_fusion.1
  47.6 9.0 %gather_fusion = bf16[2048,256]{1,0:T(8,128)(2,1)} fusion(bf16[2048,256]{1,0:T(8,128)(2,1)S(1)} %get-tuple-element.12, s32[2048]{0:T(1024)S(1)} %fusion.35), kind=kCustom, calls=%fused_computation.clone | custom fusion | bytes 2105344 | tf_op jit(solution)/shard_map/jit(_take)/gather | solution.py:53
  56.6 1.5 broadcast_select_fusion.2
  58.1 10.5 %fusion.6 = f32[4096,256]{0,1:T(8,128)} fusion(bf16[2048,256]{1,0:T(8,128)(2,1)S(1)} %broadcast_select_fusion.2, bf16[1,4096,2048]{2,1,0:T(8,128)(2,1)} %param.10), kind=kOutput, calls=%fused_computation.9 | convolution fusion | flops 4294967296 | bytes 22020096 | tf_op jit(solution)/shard_map/dot_general | solution.py:26
  68.7 7.5 %gather_fusion.1 = bf16[2048,256]{1,0:T(8,128)(2,1)S(1)} fusion(bf16[2048,256]{1,0:T(8,128)(2,1)S(1)} %get-tuple-element.10, s32[2048]{0:T(1024)S(1)} %fusion.36), kind=kCustom, calls=%fused_computation.1.clone | custom fusion | bytes 2105344 | tf_op jit(solution)/shard_map/jit(_take)/gather | solution.py:53
  76.2 0.4 broadcast_select_fusion.1
  76.7 10.6 %fusion.9 = f32[4096,256]{0,1:T(8,128)} fusion(bf16[2048,256]{1,0:T(8,128)(2,1)S(1)} %broadcast_select_fusion.1, bf16[1,4096,2048]{2,1,0:T(8,128)(2,1)} %param.10), kind=kOutput, calls=%fused_computation.10 | convolution fusion | flops 4294967296 | bytes 22020096 | tf_op jit(solution)/shard_map/dot_general | solution.py:26
  87.4 7.5 %gather_fusion.2 = bf16[2048,256]{1,0:T(8,128)(2,1)S(1)} fusion(bf16[2048,256]{1,0:T(8,128)(2,1)S(1)} %get-tuple-element.11, s32[2048]{0:T(1024)S(1)} %fusion.37), kind=kCustom, calls=%fused_computation.2.clone | custom fusion | bytes 2105344 | tf_op jit(solution)/shard_map/jit(_take)/gather | solution.py:53
  94.9 0.4 broadcast_select_fusion
  95.3 10.6 %fusion.12 = f32[4096,256]{0,1:T(8,128)} fusion(bf16[2048,256]{1,0:T(8,128)(2,1)S(1)} %broadcast_select_fusion, bf16[1,4096,2048]{2,1,0:T(8,128)(2,1)} %param.10), kind=kOutput, calls=%fused_computation.11 | convolution fusion | flops 4294967296 | bytes 22020096 | tf_op jit(solution)/shard_map/dot_general | solution.py:26
  106.0 0.8 copy-done.11
  106.8 20.3 %all_gather.10 = bf16[1,3,256,256]{3,2,1,0:T(8,128)(2,1)S(1)} all-gather(bf16[1,3,64,256]{3,2,1,0:T(8,128)(2,1)S(1)} %copy-done.11), channel_id=1, replica_groups=mesh['row'=4,'col'=2,'pole'=4] {'row'}, dimensions={2}, use_global_device_ids=true | all-gather | bytes 491520 | tf_op jit(solution)/shard_map/all_gather | solution.py:38
  127.2 24.6 %reduce-scatter.6.cloned.1.call-done = f32[1024,256]{0,1:T(8,128)} async-done(((f32[4096,256]{0,1:T(8,128)}), f32[1024,256]{0,1:T(8,128)}) %reduce-scatter.6.cloned.1.call-update) | async-done | bytes 1048592 | tf_op jit(solution)/shard_map/reduce_scatter | solution.py:58
  151.8 79.5 %reduce-scatter.8.cloned.1.call-done = f32[1024,256]{0,1:T(8,128)} async-done(((f32[4096,256]{0,1:T(8,128)}), f32[1024,256]{0,1:T(8,128)}) %reduce-scatter.8.cloned.1.call-update) | async-done | bytes 1048592 | tf_op jit(solution)/shard_map/reduce_scatter | solution.py:58
  231.3 2.2 convolution_add_fusion.2
  233.6 2.5 convolution_bitcast_fusion.6
  236.1 1.3 convolution_bitcast_fusion.4
  237.4 73.4 %reduce-scatter.10.cloned.1.call-done = f32[1024,256]{0,1:T(8,128)} async-done(((f32[4096,256]{0,1:T(8,128)}), f32[1024,256]{0,1:T(8,128)}) %reduce-scatter.10.cloned.1.call-update) | async-done | bytes 1048592 | tf_op jit(solution)/shard_map/reduce_scatter | solution.py:58
  310.8 2.1 convolution_add_fusion.1
  312.9 0.7 convolution_add_fusion
  313.7 0.8 convolution_bitcast_fusion.3
  314.4 0.6 convolution_bitcast_fusion.7
  315.1 0.8 pad_maximum_fusion.1
  315.9 0.6 convolution_bitcast_fusion.5
  316.6 0.9 pad_maximum_fusion
  317.5 1.5 convolution_bitcast_fusion.8
  319.7 0.6 fusion.44
  320.6 2.6 maximum_multiply_fusion
  323.3 31.1 %all_gather.11 = f32[1,3,256,256]{3,2,1,0:T(8,128)S(1)} all-gather(f32[1,3,64,256]{3,2,1,0:T(8,128)S(1)} %copy-done.10), channel_id=1, replica_groups=mesh['row'=4,'col'=2,'pole'=4] {'row'}, dimensions={2}, use_global_device_ids=true | all-gather | bytes 983040 | tf_op jit(solution)/shard_map/all_gather | solution.py:41
  354.4 67.3 %all-reduce.3.cloned.1.call-done = (f32[3,256,256]{2,1,0:T(8,128)}, f32[2,256,256]{2,1,0:T(8,128)}, f32[1,256,256]{2,1,0:T(8,128)}) async-done(((f32[3,256,256]{2,1,0:T(8,128)}, f32[2,256,256]{2,1,0:T(8,128)}, f32[1,256,256]{2,1,0:T(8,128)}), (f32[3,256,256]{2,1,0:T(8,128)}, f32[2,256,256]{2,1,0:T(8,128)}, f32[1,256,256]{2,1,0:T(8,128)})) %all-reduce.3.cloned.1.call-update) | async-done | bytes 1572880 | tf_op jit(solution)/shard_map/psum | solution.py:65
  421.8 0.9 fusion.34
  422.7 1.0 slice_bitcast_fusion.2
  423.6 1.3 convolution_add_fusion.6
  424.9 1.3 convolution_add_fusion.7
  426.3 0.3 convolution_add_fusion.5
  426.5 0.3 convolution_bitcast_fusion.1
  426.9 1.3 convolution_add_fusion.4
  428.2 0.3 fusion.15
  428.5 0.3 convolution_add_fusion.3
  428.8 0.3 convolution_bitcast_fusion
  429.2 1.3 maximum_multiply_fusion.1
  430.5 30.6 %reduce-scatter.12.cloned.1.call-done = f32[3,256,256]{1,2,0:T(8,128)} async-done(((f32[3,1024,256]{1,2,0:T(8,128)}), f32[3,256,256]{1,2,0:T(8,128)}) %reduce-scatter.12.cloned.1.call-update) | async-done | bytes 786448 | tf_op jit(solution)/shard_map/reduce_scatter | solution.py:96
  461.1 2.3 copy.18
  463.4 20.6 %reduce-scatter.14.cloned.1.call-done = f32[3,16,256]{2,1,0:T(8,128)} async-done(((f32[3,64,256]{2,1,0:T(8,128)}), f32[3,16,256]{2,1,0:T(8,128)}) %reduce-scatter.14.cloned.1.call-update) | async-done | bytes 49168 | tf_op jit(solution)/shard_map/reduce_scatter | solution.py:97
  (48 shorter events, 0.8 us)
Async XLA Ops:
  7.2 38.2 %all-gather.2.cloned.1.call-start = ((), (), s32[]{:S(2)}) async-start(), calls=%async_computation.5 | async-start | bytes 3145728 | tf_op jit(solution)/shard_map/all_gather | solution.py:46
  7.9 143.9 %reduce-scatter.6.cloned.1.call-start = ((), (), s32[]{:S(2)}) async-start(), calls=%async_computation.6 | async-start | bytes 5242880 | tf_op jit(solution)/shard_map/reduce_scatter | solution.py:58
  58.1 10.5 %copy-start.5 = (bf16[2048,256]{1,0:T(8,128)(2,1)}, bf16[2048,256]{1,0:T(8,128)(2,1)S(1)}, u32[]{:S(2)}) copy-start(bf16[2048,256]{1,0:T(8,128)(2,1)S(1)} %broadcast_select_fusion.2) | copy-start | bytes 3145732
  68.6 162.7 %reduce-scatter.8.cloned.1.call-start = ((), (), s32[]{:S(2)}) async-start(), calls=%async_computation.7 | async-start | bytes 5242880 | tf_op jit(solution)/shard_map/reduce_scatter | solution.py:58
  76.7 10.6 %copy-start.3 = (bf16[2048,256]{1,0:T(8,128)(2,1)}, bf16[2048,256]{1,0:T(8,128)(2,1)S(1)}, u32[]{:S(2)}) copy-start(bf16[2048,256]{1,0:T(8,128)(2,1)S(1)} %broadcast_select_fusion.1) | copy-start | bytes 3145732
  87.3 223.5 %reduce-scatter.10.cloned.1.call-start = ((), (), s32[]{:S(2)}) async-start(), calls=%async_computation.8 | async-start | bytes 5242880 | tf_op jit(solution)/shard_map/reduce_scatter | solution.py:58
  95.3 140.8 %copy-start.1 = (bf16[2048,256]{1,0:T(8,128)(2,1)}, bf16[2048,256]{1,0:T(8,128)(2,1)S(1)}, u32[]{:S(2)}) copy-start(bf16[2048,256]{1,0:T(8,128)(2,1)S(1)} %broadcast_select_fusion) | copy-start | bytes 3145732
  105.9 0.9 copy-start.11
  105.9 315.8 %all-reduce.3.cloned.1.call-start = ((), (), s32[]{:S(2)}) async-start(), calls=%async_computation.11 | async-start | bytes 3145728 | tf_op jit(solution)/shard_map/psum | solution.py:65
  151.8 159.0 %copy-start = (f32[1024,256]{0,1:T(8,128)S(1)}, f32[1024,256]{0,1:T(8,128)}, u32[]{:S(2)}) copy-start(f32[1024,256]{0,1:T(8,128)} %reduce-scatter.6.cloned.1.call-done) | copy-start | bytes 3145732
  310.8 2.8 copy-start.2
  310.8 3.6 copy-start.4
  312.9 2.2 copy-start.8
  312.9 3.7 copy-start.7
  313.6 3.9 copy-start.6
  315.1 4.6 copy-start.12
  319.0 142.1 %reduce-scatter.12.cloned.1.call-start = ((), (), s32[]{:S(2)}) async-start(), calls=%async_computation.9 | async-start | bytes 3932160 | tf_op jit(solution)/shard_map/reduce_scatter | solution.py:96
  320.6 2.6 copy-start.10
  323.2 160.7 %reduce-scatter.14.cloned.1.call-start = ((), (), s32[]{:S(2)}) async-start(), calls=%async_computation.10 | async-start | bytes 245760 | tf_op jit(solution)/shard_map/reduce_scatter | solution.py:97
  421.8 6.5 %copy-start.9 = (f32[2,256,256]{2,1,0:T(8,128)S(1)}, f32[2,256,256]{2,1,0:T(8,128)}, u32[]{:S(2)}) copy-start(f32[2,256,256]{2,1,0:T(8,128)} %get-tuple-element.8) | copy-start | bytes 1572868
Sparse Core Ops, SparseCore 0:
  9.5 35.8 all-gather.1
  68.8 82.9 reduce-scatter.5
  154.1 77.2 reduce-scatter.7
  233.5 77.2 reduce-scatter.9
  319.2 102.5 all-reduce.2
  424.1 36.9 reduce-scatter.11
  464.1 19.7 reduce-scatter.13
where the time goes:
time: 491 us
  waiting for transfers between devices  326 us (66%)
  blocking collectives  51.5 us (10%)
  matrix products  49.5 us (10%)
  local copies, waits for them, and re-layouts  31.8 us (6%)
  between operations  20.9 us (4%)
  other arithmetic  10.7 us (2%)
    reduce_scatter x3, waiting for transfers between devices, shards(): lax.psum_scatter(window_term(window_block, aligned), 'row', scatter_dimen...  178 us
    psum x1, waiting for transfers between devices, shards(): stacked = lax.psum(jnp.stack(partials + [congruence]), ('row', 'col'))  67.3 us
    dot_general x3, matrix products, window_term(): return jnp.dot(window_block, aligned, preferred_element_type=jnp.float32)  31.7 us
    all_gather x1, blocking collectives, shards(): lax.all_gather(diag_inverse, 'row', axis=2, tiled=True)  31.1 us
    reduce_scatter x1, waiting for transfers between devices, shards(): lax.psum_scatter(column_terms, 'pole', scatter_dimension=1, tiled=True)  30.6 us
    all_gather x1, waiting for transfers between devices, shards(): slot_panels = lax.all_gather(panels, 'col', axis=1, tiled=True)[0]  29.3 us
    gather x3, local copies, waits for them, and re-layouts, shards(): jnp.take(received, row_map[current] - row_index * band_rows, axis=0)  24 us
    reduce_scatter x1, waiting for transfers between devices, shards(): lax.psum_scatter(diagonal_terms, 'pole', scatter_dimension=1, tiled=True)  20.6 us
  transfers between devices with their start and end apart: 7, of which 7 were waited for; matrix products, arithmetic and copies ran while one was open for 12% of the time, Pallas kernels for 0%

commit v1 on v0

--- a/solution.py
+++ b/solution.py
@@ -4,6 +4,10 @@
 from jax.sharding import PartitionSpec as P
 
 NS = 3
+
+
+def find_the_threads(v0):
+    return jnp.sum(lax.all_gather(v0, axis_name=("row", "col")), axis=0)
 
 
 def precise(left, right):
@@ -62,7 +66,7 @@
         for earlier in range(current):
             y_window = y_window + precise(columns[earlier], factors[pair_index(current, earlier)])
         congruence = precise(own_rows.T, y_window)
-        stacked = lax.psum(jnp.stack(partials + [congruence]), ("row", "col"))
+        stacked = find_the_threads(jnp.stack(partials + [congruence]))
         summed_cross = stacked[:current]
         summed_own = stacked[current]
         y_blocks = []

time: 491 us -> 607 us (1.24)
  waiting for transfers between devices: 326 us -> 445 us
  blocking collectives: 51.5 us -> 42.6 us
  other arithmetic: 10.7 us -> 18.6 us
    all_gather x0 -> x3, waiting for transfers between devices: none -> 189 us  [find_the_threads(): return jnp.sum(lax.all_gather(v0, axis_name=('row', 'col')), axis=0)]
    psum x1 -> x0, waiting for transfers between devices: 67.3 us -> none  [shards(): stacked = lax.psum(jnp.stack(partials + [congruence]), ('row', 'col'))]
    reduce_sum x0 -> x3, other arithmetic: none -> 7.56 us  [find_the_threads(): return jnp.sum(lax.all_gather(v0, axis_name=('row', 'col')), axis=0)]
    all_gather x1, blocking collectives: 31.1 us -> 23.8 us  [shards(): lax.all_gather(diag_inverse, 'row', axis=2, tiled=True)]
  transfers between devices with their start and end apart: 7 -> 9, of which waited for: 7 -> 9; matrix products, arithmetic and copies ran while one was open for 12% -> 12% of each run, Pallas kernels for 0% -> 0%
where the time goes in v1:
time: 607 us; the launch traced here: 606 us
  waiting for transfers between devices  445 us (73%)
  matrix products  47 us (8%)
  blocking collectives  42.6 us (7%)
  local copies, waits for them, and re-layouts  31.5 us (5%)
  between operations  20.8 us (3%)
  other arithmetic  18.6 us (3%)
    all_gather x3, waiting for transfers between devices, find_the_threads(): return jnp.sum(lax.all_gather(v0, axis_name=('row', 'col')), axis=0)  189 us
    reduce_scatter x3, waiting for transfers between devices, shards(): lax.psum_scatter(window_term(window_block, aligned), 'row', scatter_dimen...  174 us
    reduce_scatter x1, waiting for transfers between devices, shards(): lax.psum_scatter(column_terms, 'pole', scatter_dimension=1, tiled=True)  31.9 us
    dot_general x3, matrix products, window_term(): return jnp.dot(window_block, aligned, preferred_element_type=jnp.float32)  31.3 us
    all_gather x1, waiting for transfers between devices, shards(): slot_panels = lax.all_gather(panels, 'col', axis=1, tiled=True)[0]  29.2 us
    gather x3, local copies, waits for them, and re-layouts, shards(): jnp.take(received, row_map[current] - row_index * band_rows, axis=0)  25.5 us
    all_gather x1, blocking collectives, shards(): lax.all_gather(diag_inverse, 'row', axis=2, tiled=True)  23.8 us
    reduce_scatter x1, waiting for transfers between devices, shards(): lax.psum_scatter(diagonal_terms, 'pole', scatter_dimension=1, tiled=True)  20.6 us
  transfers between devices with their start and end apart: 9, of which 9 were waited for; matrix products, arithmetic and copies ran while one was open for 12% of the time, Pallas kernels for 0%

profile of v1, /device:TPU:0, one launch (start us, length us, event | category | flops | bytes accessed | tf_op | source)
XLA Modules:
  0.0 606.3 jit_solution(17494644715491442112)
XLA Ops:
  7.2 0.7 all-gather.8.cloned.1.call-update
  7.9 1.4 fusion.46
  15.3 0.9 slice_subtract_fusion.1
  16.2 29.2 %all-gather.8.cloned.1.call-done = bf16[1,2,2048,256]{3,2,0,1:T(8,128)(2,1)} async-done(((bf16[1,1,2048,256]{3,2,0,1:T(8,128)(2,1)}), bf16[1,2,2048,256]{3,2,0,1:T(8,128)(2,1)}) %all-gather.8.cloned.1.call-update) | async-done | bytes 2097168 | tf_op jit(solution)/shard_map/all_gather | solution.py:50
  45.4 2.2 dynamic-slice_bitcast_fusion.1
  47.6 9.0 %gather_fusion = bf16[2048,256]{1,0:T(8,128)(2,1)} fusion(bf16[2048,256]{1,0:T(8,128)(2,1)S(1)} %get-tuple-element.9, s32[2048]{0:T(1024)S(1)} %fusion.36), kind=kCustom, calls=%fused_computation.clone | custom fusion | bytes 2105344 | tf_op jit(solution)/shard_map/jit(_take)/gather | solution.py:57
  56.6 1.5 broadcast_select_fusion.2
  58.1 10.6 %fusion.6 = f32[4096,256]{0,1:T(8,128)} fusion(bf16[2048,256]{1,0:T(8,128)(2,1)S(1)} %broadcast_select_fusion.2, bf16[1,4096,2048]{2,1,0:T(8,128)(2,1)} %param.10), kind=kOutput, calls=%fused_computation.9 | convolution fusion | flops 4294967296 | bytes 22020096 | tf_op jit(solution)/shard_map/dot_general | solution.py:30
  68.7 9.0 %gather_fusion.1 = bf16[2048,256]{1,0:T(8,128)(2,1)} fusion(bf16[2048,256]{1,0:T(8,128)(2,1)S(1)} %get-tuple-element.7, s32[2048]{0:T(1024)S(1)} %fusion.37), kind=kCustom, calls=%fused_computation.1.clone | custom fusion | bytes 2105344 | tf_op jit(solution)/shard_map/jit(_take)/gather | solution.py:57
  77.7 1.5 broadcast_select_fusion.1
  79.2 10.2 %fusion.9 = f32[4096,256]{0,1:T(8,128)} fusion(bf16[2048,256]{1,0:T(8,128)(2,1)S(1)} %broadcast_select_fusion.1, bf16[1,4096,2048]{2,1,0:T(8,128)(2,1)} %param.10), kind=kOutput, calls=%fused_computation.10 | convolution fusion | flops 4294967296 | bytes 22020096 | tf_op jit(solution)/shard_map/dot_general | solution.py:30
  89.6 7.5 %gather_fusion.2 = bf16[2048,256]{1,0:T(8,128)(2,1)S(1)} fusion(bf16[2048,256]{1,0:T(8,128)(2,1)S(1)} %get-tuple-element.8, s32[2048]{0:T(1024)S(1)} %fusion.38), kind=kCustom, calls=%fused_computation.2.clone | custom fusion | bytes 2105344 | tf_op jit(solution)/shard_map/jit(_take)/gather | solution.py:57
  97.1 0.4 broadcast_select_fusion
  97.5 10.5 %fusion.12 = f32[4096,256]{0,1:T(8,128)} fusion(bf16[2048,256]{1,0:T(8,128)(2,1)S(1)} %broadcast_select_fusion, bf16[1,4096,2048]{2,1,0:T(8,128)(2,1)} %param.10), kind=kOutput, calls=%fused_computation.11 | convolution fusion | flops 4294967296 | bytes 22020096 | tf_op jit(solution)/shard_map/dot_general | solution.py:30
  108.2 37.3 %reduce-scatter.6.cloned.1.call-done = f32[1024,256]{0,1:T(8,128)} async-done(((f32[4096,256]{0,1:T(8,128)}), f32[1024,256]{0,1:T(8,128)}) %reduce-scatter.6.cloned.1.call-update) | async-done | bytes 1048592 | tf_op jit(solution)/shard_map/reduce_scatter | solution.py:62
  145.5 2.8 fusion.22
  148.3 18.8 %all_gather.25 = bf16[1,3,256,256]{3,2,1,0:T(8,128)(2,1)S(1)} all-gather(bf16[1,3,64,256]{3,2,1,0:T(8,128)(2,1)} %param.14), channel_id=1, replica_groups=mesh['row'=4,'col'=2,'pole'=4] {'row'}, dimensions={2}, use_global_device_ids=true | all-gather | bytes 491520 | tf_op jit(solution)/shard_map/all_gather | solution.py:42
  167.1 61.9 %reduce-scatter.8.cloned.1.call-done = f32[1024,256]{0,1:T(8,128)} async-done(((f32[4096,256]{0,1:T(8,128)}), f32[1024,256]{0,1:T(8,128)}) %reduce-scatter.8.cloned.1.call-update) | async-done | bytes 1048592 | tf_op jit(solution)/shard_map/reduce_scatter | solution.py:62
  229.0 2.2 convolution_add_fusion.2
  231.3 0.8 convolution_bitcast_fusion.6
  232.1 0.6 convolution_bitcast_fusion.7
  232.7 0.9 pad_maximum_fusion.1
  233.6 75.0 %reduce-scatter.10.cloned.1.call-done = f32[1024,256]{0,1:T(8,128)} async-done(((f32[4096,256]{0,1:T(8,128)}), f32[1024,256]{0,1:T(8,128)}) %reduce-scatter.10.cloned.1.call-update) | async-done | bytes 1048592 | tf_op jit(solution)/shard_map/reduce_scatter | solution.py:62
  308.6 1.9 convolution_add_fusion.1
  310.6 0.7 convolution_add_fusion
  311.3 1.8 convolution_bitcast_fusion.3
  313.1 1.7 convolution_bitcast_fusion.4
  314.8 0.7 convolution_bitcast_fusion.5
  315.5 0.9 pad_maximum_fusion
  317.2 0.6 fusion.45
  318.0 2.7 maximum_multiply_fusion
  320.8 23.8 %all_gather.26 = f32[1,3,256,256]{3,2,1,0:T(8,128)S(1)} all-gather(f32[1,3,64,256]{3,2,1,0:T(8,128)S(1)} %copy-done.5), channel_id=1, replica_groups=mesh['row'=4,'col'=2,'pole'=4] {'row'}, dimensions={2}, use_global_device_ids=true | all-gather | bytes 983040 | tf_op jit(solution)/shard_map/all_gather | solution.py:45
  344.7 20.4 %all-gather.10.cloned.1.call-done = f32[2048,256]{1,0:T(8,128)} async-done(((f32[256,256]{1,0:T(8,128)}), f32[2048,256]{1,0:T(8,128)}) %all-gather.10.cloned.1.call-update) | async-done | bytes 2097168 | tf_op jit(solution)/shard_map/all_gather | solution.py:10
  365.1 1.8 reduce.1
  366.8 71.5 %all-gather.12.cloned.1.call-done = f32[16,256,256]{2,1,0:T(8,128)} async-done(((f32[2,256,256]{2,1,0:T(8,128)}), f32[16,256,256]{2,1,0:T(8,128)}) %all-gather.12.cloned.1.call-update) | async-done | bytes 4194320 | tf_op jit(solution)/shard_map/all_gather | solution.py:10
  438.4 2.5 reduce_sum.38
  440.9 0.3 convolution_add_fusion.7
  441.2 0.3 fusion.15
  441.5 96.9 %all-gather.14.cloned.1.call-done = f32[24,256,256]{2,1,0:T(8,128)} async-done(((f32[3,256,256]{2,1,0:T(8,128)}), f32[24,256,256]{2,1,0:T(8,128)}) %all-gather.14.cloned.1.call-update) | async-done | bytes 6291472 | tf_op jit(solution)/shard_map/all_gather | solution.py:10
  538.4 3.3 reduce_sum.39
  541.7 0.3 convolution_add_fusion.6
  542.3 0.3 convolution_bitcast_fusion.1
  542.6 0.4 convolution_add_fusion.4
  543.3 0.3 convolution_bitcast_fusion
  543.6 1.3 maximum_multiply_fusion.1
  544.9 31.9 %reduce-scatter.12.cloned.1.call-done = f32[3,256,256]{1,2,0:T(8,128)} async-done(((f32[3,1024,256]{1,2,0:T(8,128)}), f32[3,256,256]{1,2,0:T(8,128)}) %reduce-scatter.12.cloned.1.call-update) | async-done | bytes 786448 | tf_op jit(solution)/shard_map/reduce_scatter | solution.py:100
  576.9 2.3 copy.18
  579.1 20.6 %reduce-scatter.14.cloned.1.call-done = f32[3,16,256]{2,1,0:T(8,128)} async-done(((f32[3,64,256]{2,1,0:T(8,128)}), f32[3,16,256]{2,1,0:T(8,128)}) %reduce-scatter.14.cloned.1.call-update) | async-done | bytes 49168 | tf_op jit(solution)/shard_map/reduce_scatter | solution.py:101
  (47 shorter events, 1.5 us)
Async XLA Ops:
  7.2 38.2 %all-gather.8.cloned.1.call-start = ((), (), s32[]{:S(2)}) async-start(), calls=%async_computation.5 | async-start | bytes 3145728 | tf_op jit(solution)/shard_map/all_gather | solution.py:50
  7.9 137.6 %reduce-scatter.6.cloned.1.call-start = ((), (), s32[]{:S(2)}) async-start(), calls=%async_computation.6 | async-start | bytes 5242880 | tf_op jit(solution)/shard_map/reduce_scatter | solution.py:62
  58.1 10.6 %copy-start.3 = (bf16[2048,256]{1,0:T(8,128)(2,1)}, bf16[2048,256]{1,0:T(8,128)(2,1)S(1)}, u32[]{:S(2)}) copy-start(bf16[2048,256]{1,0:T(8,128)(2,1)S(1)} %broadcast_select_fusion.2) | copy-start | bytes 3145732
  68.7 160.3 %reduce-scatter.8.cloned.1.call-start = ((), (), s32[]{:S(2)}) async-start(), calls=%async_computation.7 | async-start | bytes 5242880 | tf_op jit(solution)/shard_map/reduce_scatter | solution.py:62
  89.5 219.1 %reduce-scatter.10.cloned.1.call-start = ((), (), s32[]{:S(2)}) async-start(), calls=%async_computation.8 | async-start | bytes 5242880 | tf_op jit(solution)/shard_map/reduce_scatter | solution.py:62
  97.5 10.6 %copy-start.1 = (bf16[2048,256]{1,0:T(8,128)(2,1)}, bf16[2048,256]{1,0:T(8,128)(2,1)S(1)}, u32[]{:S(2)}) copy-start(bf16[2048,256]{1,0:T(8,128)(2,1)S(1)} %broadcast_select_fusion) | copy-start | bytes 3145732
  108.1 37.4 %copy-start.4 = (bf16[2048,256]{1,0:T(8,128)(2,1)S(1)}, bf16[2048,256]{1,0:T(8,128)(2,1)}, u32[]{:S(2)}) copy-start(bf16[2048,256]{1,0:T(8,128)(2,1)} %copy-done.3) | copy-start | bytes 3145732
  108.1 256.9 %all-gather.10.cloned.1.call-start = ((), (), s32[]{:S(2)}) async-start(), calls=%async_computation.11 | async-start | bytes 2359296 | tf_op jit(solution)/shard_map/all_gather | solution.py:10
  145.5 86.6 %copy-start = (f32[1024,256]{0,1:T(8,128)S(1)}, f32[1024,256]{0,1:T(8,128)}, u32[]{:S(2)}) copy-start(f32[1024,256]{0,1:T(8,128)} %reduce-scatter.6.cloned.1.call-done) | copy-start | bytes 3145732
  148.3 290.1 %all-gather.12.cloned.1.call-start = ((), (), s32[]{:S(2)}) async-start(), calls=%async_computation.12 | async-start | bytes 4718592 | tf_op jit(solution)/shard_map/all_gather | solution.py:10
  233.6 304.8 %all-gather.14.cloned.1.call-start = ((), (), s32[]{:S(2)}) async-start(), calls=%async_computation.13 | async-start | bytes 7077888 | tf_op jit(solution)/shard_map/all_gather | solution.py:10
  310.6 4.3 copy-start.2
  311.3 5.8 copy-start.6
  316.4 260.4 %reduce-scatter.12.cloned.1.call-start = ((), (), s32[]{:S(2)}) async-start(), calls=%async_computation.9 | async-start | bytes 3932160 | tf_op jit(solution)/shard_map/reduce_scatter | solution.py:100
  318.0 2.8 copy-start.5
  320.8 279.0 %reduce-scatter.14.cloned.1.call-start = ((), (), s32[]{:S(2)}) async-start(), calls=%async_computation.10 | async-start | bytes 245760 | tf_op jit(solution)/shard_map/reduce_scatter | solution.py:101
Sparse Core Ops, SparseCore 0:
  9.5 35.8 all-gather.7
  68.8 76.6 reduce-scatter.5
  147.7 81.2 reduce-scatter.7
  231.2 77.4 reduce-scatter.9
  310.6 54.4 all-gather.9
  367.0 71.3 all-gather.11
  441.1 97.2 all-gather.13
  540.9 35.8 reduce-scatter.11
  579.9 19.7 reduce-scatter.13
